TPU v7x, 32 devices: a whole 2x2x4 slice. The times are simulated.
32 devices in a mesh: mp: 2 (over x), width: 2 (over y), hidden: 8 (over z, core).
Axes of the slice: x: 2, y: 2, z: 4, core: 2. Of those that a mesh axis runs over, the one named last changes fastest.
Arguments:
- residual_in: bfloat16 [2, 512, 3584], P('mp', 'hidden'), may hold values from -6 to 6
- gate_weight: bfloat16 [2, 14336, 3584], P('mp', ('width', 'hidden')), may hold values from -0.09375 to 0.09375
- up_weight: bfloat16 [2, 14336, 3584], P('mp', ('width', 'hidden')), may hold values from -0.09375 to 0.09375
- down_weight: bfloat16 [2, 14336, 3584], P('mp', ('width', 'hidden')), may hold values from -0.046875 to 0.046875
- enc_weight: float32 [7168, 16384], P(('mp', 'width'), 'hidden'), may hold values from -0.0625 to 0.0625
- enc_bias: float32 [16384], P('hidden'), may hold values from -3 to 3
- dec_weight: float32 [16384, 7168], P('hidden', ('mp', 'width')), may hold values from -0.25 to 0.25
- dec_bias: float32 [7168], P(('mp', 'width')), may hold values from -2 to 2
Outputs:
- mlp_acts: bfloat16 [2, 512, 3584], P('mp', 'hidden', 'width')
- latents: float32 [512, 16384], P(None, 'hidden')
- grad_enc: float32 [7168, 16384], P(('mp', 'width'), 'hidden')
- grad_dec: float32 [16384, 7168], P('hidden', ('mp', 'width'))
- grad_enc_bias: float32 [16384], P('hidden')
- grad_dec_bias: float32 [7168], P(('mp', 'width'))
All inputs are finite; a program needn't handle non-finite values.
Results may differ from a plain program's by a relative error of at most 0.0058.
Values may be sent and summed in bfloat16 or wider, within the bound.
A program may use at most 192 MiB of HBM per device.

v0:
```python
import jax
import jax.numpy as jnp
from jax import lax
from jax.sharding import PartitionSpec as P

TOKENS = 512
sharpness = 8.0
sparsity_coef = 0.02
norm_floor = 1e-06
highest = lax.Precision.HIGHEST


def body(
    residual_in, gate_weight, up_weight, down_weight, enc_weight, enc_bias, dec_weight, dec_bias
):
    last_last = (((1,), (1,)), ((), ()))
    first_first = (((0,), (0,)), ((), ()))
    gathered = lax.all_gather(residual_in[0], "hidden", axis=0, tiled=True)
    gate_act = lax.dot_general(
        gathered, gate_weight[0], last_last, preferred_element_type=jnp.float32
    )
    up_act = lax.dot_general(gathered, up_weight[0], last_last, preferred_element_type=jnp.float32)
    hidden_act = (jax.nn.gelu(gate_act, approximate=True) * up_act).astype(jnp.bfloat16)
    down_local = down_weight[0]
    row_sums = lax.psum_scatter(
        jnp.dot(hidden_act, down_local, preferred_element_type=jnp.float32),
        "hidden",
        scatter_dimension=0,
        tiled=True,
    )
    model_sums = lax.psum_scatter(row_sums, "width", scatter_dimension=1, tiled=True)
    mlp_acts = model_sums.astype(jnp.bfloat16)
    coder_in = lax.all_gather(mlp_acts, "hidden", axis=0, tiled=True).astype(jnp.float32)
    enc_partial = jnp.dot(coder_in, enc_weight, precision=highest)
    model_index = lax.axis_index("mp")
    squares = jnp.sum(dec_weight * dec_weight, axis=1)
    square_pair = jnp.where(jnp.arange(2)[:, None] == model_index, squares[None, :], 0.0)
    pre_sum, square_sums = lax.psum((enc_partial, square_pair), ("mp", "width"))
    pre_act = pre_sum + enc_bias
    latents = jax.nn.softplus(sharpness * pre_act) / sharpness
    dec_norms = jnp.sqrt(square_sums + norm_floor)
    recon_part = jnp.dot(latents, dec_weight, precision=highest)
    own_rebuilt = lax.psum_scatter(recon_part, "hidden", scatter_dimension=0, tiled=True) + dec_bias
    own_grad = 2.0 / TOKENS * (own_rebuilt - mlp_acts.astype(jnp.float32))
    err_grad = lax.all_gather(own_grad.astype(jnp.bfloat16), "hidden", axis=0, tiled=True).astype(
        own_grad.dtype
    )
    grad_dec_bias = jnp.sum(err_grad, axis=0)
    back_part = lax.dot_general(
        err_grad, dec_weight, last_last, precision=highest, preferred_element_type=jnp.float32
    )
    lat_grad = lax.psum(back_part.astype(jnp.bfloat16), ("mp", "width")).astype(
        jnp.float32
    ) + sparsity_coef * (dec_norms[0] + dec_norms[1])
    pre_grad = lat_grad * jax.nn.sigmoid(sharpness * pre_act)
    grad_enc_bias = jnp.sum(pre_grad, axis=0)
    grad_enc = lax.dot_general(
        coder_in, pre_grad, first_first, precision=highest, preferred_element_type=jnp.float32
    )
    latent_totals = jnp.sum(latents, axis=0)
    own_norm = jnp.where(model_index == 0, dec_norms[0], dec_norms[1])
    grad_dec = lax.dot_general(
        latents, err_grad, first_first, precision=highest, preferred_element_type=jnp.float32
    )
    grad_dec = grad_dec + sparsity_coef * (latent_totals / own_norm)[:, None] * dec_weight
    return (mlp_acts[None], latents, grad_enc, grad_dec, grad_enc_bias, grad_dec_bias)


def solution(mesh):
    return jax.shard_map(
        body,
        mesh=mesh,
        in_specs=(
            P("mp", "hidden", None),
            P("mp", ("width", "hidden"), None),
            P("mp", ("width", "hidden"), None),
            P("mp", ("width", "hidden"), None),
            P(("mp", "width"), "hidden"),
            P("hidden"),
            P("hidden", ("mp", "width")),
            P(("mp", "width")),
        ),
        out_specs=(
            P("mp", "hidden", "width"),
            P(None, "hidden"),
            P(("mp", "width"), "hidden"),
            P("hidden", ("mp", "width")),
            P("hidden"),
            P(("mp", "width")),
        ),
        check_vma=False,
    )
```

profile of v0, /device:TPU:0, one launch (start us, length us, event | category | flops | bytes accessed | tf_op | source)
XLA Modules:
  0.0 549.1 jit_solution(14673929088239518730)
XLA Ops:
  7.2 0.0 all-gather.9.cloned.1.call-start
  7.2 0.7 all-gather.9.cloned.1.call-update
  7.9 0.0 reduce-scatter.4.cloned.1.call-start
  7.9 47.0 %all-gather.9.cloned.1.call-done = bf16[1,512,3584]{2,1,0:T(8,128)(2,1)} async-done(((bf16[1,64,3584]{2,1,0:T(8,128)(2,1)}), bf16[1,512,3584]{2,1,0:T(8,128)(2,1)}) %all-gather.9.cloned.1.call-update) | async-done | bytes 3670032 | tf_op jit(solution)/shard_map/all_gather | solution.py:18
  54.9 9.6 %fusion.4 = f32[512,896]{1,0:T(8,128)S(1)} fusion(bf16[1,896,3584]{2,1,0:T(8,128)(2,1)} %param.9, bf16[1,512,3584]{2,1,0:T(8,128)(2,1)} %all-gather.9.cloned.1.call-done), kind=kOutput, calls=%fused_computation.7 | convolution fusion | flops 3288334336 | bytes 11927552 | tf_op jit(solution)/shard_map/dot_general | solution.py:19
  64.5 0.0 copy-done.7
  64.6 0.0 slice-start.1
  64.6 7.1 %fusion.17 = bf16[512,896]{1,0:T(8,128)(2,1)S(1)} fusion(f32[512,896]{1,0:T(8,128)S(1)} %fusion.4, bf16[1,896,3584]{2,1,0:T(8,128)(2,1)} %param.10, bf16[1,512,3584]{2,1,0:T(8,128)(2,1)S(1)} %copy-done.7), kind=kOutput, calls=%fused_computation.25 | convolution fusion | flops 3292921856 | bytes 12845056 | tf_op jit(solution)/shard_map/dot_general | solution.py:22
  71.7 0.0 slice-done
  71.7 0.0 slice-done.1
  71.7 6.0 %fusion = f32[512,3584]{1,0:T(8,128)} fusion(bf16[512,896]{1,0:T(8,128)(2,1)S(1)} %fusion.17, bf16[1,896,3584]{2,1,0:T(8,128)(2,1)S(1)} %bitcast.36), kind=kOutput, calls=%fused_computation.3 | convolution fusion | flops 3288334336 | bytes 14680064 | tf_op jit(solution)/shard_map/dot_general | solution.py:26
  77.8 0.0 reduce-scatter.4.cloned.1.call-update
  77.8 0.0 reduce-scatter.6.cloned.1.call-start
  77.9 78.6 %reduce-scatter.4.cloned.1.call-done = f32[64,3584]{1,0:T(8,128)} async-done(((f32[512,3584]{1,0:T(8,128)}), f32[64,3584]{1,0:T(8,128)}) %reduce-scatter.4.cloned.1.call-update) | async-done | bytes 917520 | tf_op jit(solution)/shard_map/reduce_scatter | solution.py:25
  156.4 0.0 reduce-scatter.6.cloned.1.call-update
  156.4 0.0 all-gather.5.cloned.1.call-start
  156.5 19.6 %reduce-scatter.6.cloned.1.call-done = f32[64,1792]{1,0:T(8,128)} async-done(((f32[64,3584]{1,0:T(8,128)}), f32[64,1792]{1,0:T(8,128)}) %reduce-scatter.6.cloned.1.call-update) | async-done | bytes 458768 | tf_op jit(solution)/shard_map/reduce_scatter | solution.py:31
  176.1 1.7 convert_element_type.23
  177.8 0.0 all-gather.5.cloned.1.call-update
  177.9 0.3 all-reduce.3.cloned.1.call-start
  178.2 27.0 %all-gather.5.cloned.1.call-done = bf16[512,1792]{1,0:T(8,128)(2,1)} async-done(((bf16[64,1792]{1,0:T(8,128)(2,1)}), bf16[512,1792]{1,0:T(8,128)(2,1)}) %all-gather.5.cloned.1.call-update) | async-done | bytes 1835024 | tf_op jit(solution)/shard_map/all_gather | solution.py:33
  205.2 16.9 %fusion.26 = f32[512,2048]{1,0:T(8,128)} fusion(bf16[512,1792]{1,0:T(8,128)(2,1)} %all-gather.5.cloned.1.call-done, f32[1792,2048]{1,0:T(8,128)} %param.12), kind=kOutput, calls=%fused_computation.36 | convolution fusion | flops 22548578304 | bytes 20709376 | tf_op jit(solution)/shard_map/dot_general | solution.py:34
  222.1 0.0 all-reduce.3.cloned.1.call-update
  222.1 0.4 reduce-scatter.8.cloned.1.call-start
  222.5 102.8 %all-reduce.3.cloned.1.call-done = f32[512,2048]{1,0:T(8,128)} async-done(((f32[512,2048]{1,0:T(8,128)}), f32[512,2048]{1,0:T(8,128)}) %all-reduce.3.cloned.1.call-update) | async-done | bytes 4194320 | tf_op jit(solution)/shard_map/psum | solution.py:38
  325.3 4.9 fusion.24
  330.2 0.0 copy-start
  330.2 2.0 copy-done
  332.2 26.6 %fusion.27 = f32[512,1792]{1,0:T(8,128)} fusion(f32[512,2048]{1,0:T(8,128)S(1)} %get-tuple-element.7, f32[2048,1792]{1,0:T(8,128)} %param.14), kind=kOutput, calls=%fused_computation.37 | convolution fusion | flops 22548578304 | bytes 22544384 | tf_op jit(solution)/shard_map/dot_general | solution.py:42
  358.9 0.0 reduce-scatter.8.cloned.1.call-update
  358.9 0.0 all-gather.7.cloned.1.call-start
  359.0 45.1 %reduce-scatter.8.cloned.1.call-done = f32[64,1792]{1,0:T(8,128)} async-done(((f32[512,1792]{1,0:T(8,128)}), f32[64,1792]{1,0:T(8,128)}) %reduce-scatter.8.cloned.1.call-update) | async-done | bytes 458768 | tf_op jit(solution)/shard_map/reduce_scatter | solution.py:43
  404.0 0.0 copy-done.6
  404.1 1.8 multiply_convert_fusion
  405.8 0.0 all-gather.7.cloned.1.call-update
  405.8 0.0 all-reduce.5.cloned.1.call-start
  405.9 6.2 %multiply_reduce_fusion = f32[2048]{0:T(1024)S(1)} fusion(f32[2048,1792]{1,0:T(8,128)} %param.14), kind=kLoop, calls=%fused_computation.1 | loop fusion | flops 7337984 | bytes 14688256 | tf_op jit(solution)/shard_map/reduce_sum | solution.py:36
  412.1 0.1 broadcast_select_fusion
  412.2 16.5 %psum.23 = f32[2,2048]{1,0:T(2,128)S(1)} all-reduce(f32[2,2048]{1,0:T(2,128)S(1)} %broadcast_select_fusion), channel_id=1, replica_groups=mesh['mp'=2,'width'=2,'hidden'=8] {'mp','width'}, use_global_device_ids=true, to_apply=%region_6.7 | all-reduce | flops 4096 | bytes 32768 | tf_op jit(solution)/shard_map/psum | solution.py:38
  428.8 2.9 all-gather.7.cloned.1.call-done
  431.7 18.4 %convolution_convert_fusion = bf16[512,2048]{1,0:T(8,128)(2,1)} fusion(bf16[512,1792]{1,0:T(8,128)(2,1)} %all-gather.7.cloned.1.call-done, f32[2048,1792]{1,0:T(8,128)} %param.14), kind=kOutput, calls=%fused_computation.15 | convolution fusion | flops 22549626880 | bytes 18612224 | tf_op jit(solution)/shard_map/dot_general | solution.py:49
  450.1 0.0 all-reduce.5.cloned.1.call-update
  450.1 0.7 convert_bitcast_fusion
  450.8 0.9 convert_reduce_fusion
  451.7 19.6 %multiply_add_fusion = f32[2048,1792]{1,0:T(8,128)} fusion(f32[2048,1792]{1,0:T(8,128)} %param.14, f32[512,2048]{1,0:T(8,128)} %copy-done, bf16[512,1792]{1,0:T(8,128)(2,1)S(1)} %copy-done.2, f32[2048]{0:T(1024)S(1)} %divide_multiply_fusion.1), kind=kOutput, calls=%fused_computation | convolution fusion | flops 22555918336 | bytes 35397632 | tf_op jit(solution)/shard_map/dot_general | solution.py:62
  471.3 47.8 %all-reduce.5.cloned.1.call-done = bf16[512,2048]{1,0:T(8,128)(2,1)} async-done(((bf16[512,2048]{1,0:T(8,128)(2,1)}), bf16[512,2048]{1,0:T(8,128)(2,1)}) %all-reduce.5.cloned.1.call-update) | async-done | bytes 2097168 | tf_op jit(solution)/shard_map/psum | solution.py:52
  519.2 5.0 fusion.22
  524.1 17.9 %fusion.23 = f32[1792,2048]{1,0:T(8,128)} fusion(bf16[512,1792]{1,0:T(8,128)(2,1)} %all-gather.5.cloned.1.call-done, bf16[512,2048]{1,0:T(8,128)(2,1)S(1)} %copy-done.4, f32[512,2048]{1,0:T(8,128)S(1)} %copy-done.1, f32[2048]{0:T(1024)S(1)} %bitcast.33, f32[2048]{0:T(1024)S(1)} %copy-done.5), kind=kOutput, calls=%fused_computation.34 | convolution fusion | flops 22556966912 | bytes 22822912 | tf_op jit(solution)/shard_map/dot_general | solution.py:57
  (18 shorter events, 0.1 us)
Async XLA Ops:
  7.2 47.7 %all-gather.9.cloned.1.call-start = ((), (), s32[]{:S(2)}) async-start(), calls=%async_computation.10 | async-start | bytes 4128768 | tf_op jit(solution)/shard_map/all_gather | solution.py:18
  7.9 148.5 %reduce-scatter.4.cloned.1.call-start = ((), (), s32[]{:S(2)}) async-start(), calls=%async_computation.3 | async-start | bytes 8257536 | tf_op jit(solution)/shard_map/reduce_scatter | solution.py:25
  54.9 9.6 %copy-start.7 = (bf16[1,512,3584]{2,1,0:T(8,128)(2,1)S(1)}, bf16[1,512,3584]{2,1,0:T(8,128)(2,1)}, u32[]{:S(2)}) copy-start(bf16[1,512,3584]{2,1,0:T(8,128)(2,1)} %all-gather.9.cloned.1.call-done) | copy-start | bytes 11010052
  54.9 16.8 %slice-start = ((s8[6422528]{0:T(1024)(128)(4,1)}), s8[4194304]{0:T(1024)(128)(4,1)S(1)}, s32[]{:S(2)}) async-start(s8[6422528]{0:T(1024)(128)(4,1)} %bitcast.35), calls=%async_computation.11 | async-start | bytes 8388608
  64.6 7.2 %slice-start.1 = ((s8[6422528]{0:T(1024)(128)(4,1)}), s8[2228224]{0:T(1024)(128)(4,1)S(1)}, s32[]{:S(2)}) async-start(s8[6422528]{0:T(1024)(128)(4,1)} %bitcast.35), calls=%async_computation.12 | async-start | bytes 4456448
  77.8 98.3 %reduce-scatter.6.cloned.1.call-start = ((), (), s32[]{:S(2)}) async-start(), calls=%async_computation.4 | async-start | bytes 1376256 | tf_op jit(solution)/shard_map/reduce_scatter | solution.py:31
  156.4 48.8 %all-gather.5.cloned.1.call-start = ((), (), s32[]{:S(2)}) async-start(), calls=%async_computation.5 | async-start | bytes 2064384 | tf_op jit(solution)/shard_map/all_gather | solution.py:33
  177.9 147.4 %all-reduce.3.cloned.1.call-start = ((), (), s32[]{:S(2)}) async-start(), calls=%async_computation.6 | async-start | bytes 8388608 | tf_op jit(solution)/shard_map/psum | solution.py:38
  222.1 103.2 %copy-start.5 = (f32[2048]{0:T(1024)S(1)}, f32[2048]{0:T(1024)}, u32[]{:S(2)}) copy-start(f32[2048]{0:T(1024)} %param.13) | copy-start | bytes 24580
  222.1 181.9 %reduce-scatter.8.cloned.1.call-start = ((), (), s32[]{:S(2)}) async-start(), calls=%async_computation.7 | async-start | bytes 4128768 | tf_op jit(solution)/shard_map/reduce_scatter | solution.py:43
  330.2 2.0 copy-start
  332.2 71.8 %copy-start.3 = (f32[64,1792]{1,0:T(8,128)S(1)}, f32[64,1792]{1,0:T(8,128)}, u32[]{:S(2)}) copy-start(f32[64,1792]{1,0:T(8,128)} %reduce-scatter.6.cloned.1.call-done) | copy-start | bytes 1376260
  332.2 71.8 %copy-start.6 = (f32[1792]{0:T(1024)S(1)}, f32[1792]{0:T(1024)}, u32[]{:S(2)}) copy-start(f32[1792]{0:T(1024)} %param.15) | copy-start | bytes 21508
  358.9 72.7 %all-gather.7.cloned.1.call-start = ((), (), s32[]{:S(2)}) async-start(), calls=%async_computation.8 | async-start | bytes 2064384 | tf_op jit(solution)/shard_map/all_gather | solution.py:45
  405.8 113.3 %all-reduce.5.cloned.1.call-start = ((), (), s32[]{:S(2)}) async-start(), calls=%async_computation.9 | async-start | bytes 4194304 | tf_op jit(solution)/shard_map/psum | solution.py:52
  431.7 19.2 %copy-start.2 = (bf16[512,1792]{1,0:T(8,128)(2,1)S(1)}, bf16[512,1792]{1,0:T(8,128)(2,1)}, u32[]{:S(2)}) copy-start(bf16[512,1792]{1,0:T(8,128)(2,1)} %all-gather.7.cloned.1.call-done) | copy-start | bytes 5505028
  519.1 5.0 copy-start.1
  519.1 5.0 copy-start.4
Sparse Core Ops, SparseCore 0:
  9.6 45.2 all-gather.8
  77.9 78.4 reduce-scatter.3
  158.7 17.3 reduce-scatter.5
  178.2 26.9 all-gather.4
  222.2 103.0 all-reduce.2
  359.0 44.9 reduce-scatter.7
  406.3 25.3 all-gather.6
  450.2 68.8 all-reduce.4
where the time goes:
time: 555 us; the launch traced here: 549 us
  waiting for transfers between devices  372 us (67%)
  matrix products  122 us (22%)
  other arithmetic  21.3 us (4%)
  blocking collectives  16.5 us (3%)
  between operations  14.5 us (3%)
    psum x1, waiting for transfers between devices, body(): pre_sum, square_sums = lax.psum((enc_partial, square_pair), ('mp', 'width'))  103 us
    reduce_scatter x1, waiting for transfers between devices, body(): lax.psum_scatter(jnp.dot(hidden_act, down_local, preferred_element_type=j...  78.6 us
    psum x1, waiting for transfers between devices, body(): lax.psum(back_part.astype(jnp.bfloat16), ('mp', 'width'))  47.8 us
    all_gather x1, waiting for transfers between devices, body(): gathered = lax.all_gather(residual_in[0], 'hidden', axis=0, tiled=True)  47 us
    reduce_scatter x1, waiting for transfers between devices, body(): lax.psum_scatter(recon_part, 'hidden', scatter_dimension=0, tiled=True)  45.1 us
    all_gather x1, waiting for transfers between devices, body(): lax.all_gather(mlp_acts, 'hidden', axis=0, tiled=True).astype(jnp.float32)  27 us
    dot_general x1, matrix products, body(): recon_part = jnp.dot(latents, dec_weight, precision=highest)  26.6 us
    reduce_scatter x1, waiting for transfers between devices, body(): lax.psum_scatter(row_sums, 'width', scatter_dimension=1, tiled=True)  19.6 us
  transfers between devices with their start and end apart: 8, of which 8 were waited for; matrix products, arithmetic and copies ran while one was open for 5% of the time, Pallas kernels for 0%

commit v1 on v0

--- a/solution.py
+++ b/solution.py
@@ -35,7 +35,7 @@
     model_index = lax.axis_index("mp")
     squares = jnp.sum(dec_weight * dec_weight, axis=1)
     square_pair = jnp.where(jnp.arange(2)[:, None] == model_index, squares[None, :], 0.0)
-    pre_sum, square_sums = lax.psum((enc_partial, square_pair), ("mp", "width"))
+    pre_sum, square_sums = lax.psum(lax.psum((enc_partial, square_pair), "mp"), "width")
     pre_act = pre_sum + enc_bias
     latents = jax.nn.softplus(sharpness * pre_act) / sharpness
     dec_norms = jnp.sqrt(square_sums + norm_floor)

time: 555 us -> 669 us (1.21)
  waiting for transfers between devices: 372 us -> 486 us
    psum x1 -> x2, waiting for transfers between devices: 103 us -> 217 us  [the longest x1 110 us: body(): lax.psum(lax.psum((enc_partial, square_pair), 'mp'), 'width')]
    psum x1 -> x2, blocking collectives: 16.5 us -> 16.8 us  [the longest x1 8.68 us: body(): lax.psum(lax.psum((enc_partial, square_pair), 'mp'), 'width')]
  transfers between devices with their start and end apart: 8 -> 9, of which waited for: 8 -> 9; matrix products, arithmetic and copies ran while one was open for 5% -> 4% of each run, Pallas kernels for 0% -> 0%
where the time goes in v1:
time: 669 us; the launch traced here: 663 us
  waiting for transfers between devices  486 us (73%)
  matrix products  122 us (18%)
  other arithmetic  21.3 us (3%)
  blocking collectives  16.8 us (3%)
  between operations  14.2 us (2%)
    psum x1, waiting for transfers between devices, body(): lax.psum(lax.psum((enc_partial, square_pair), 'mp'), 'width')  110 us
    psum x1, waiting for transfers between devices, body(): lax.psum((enc_partial, square_pair), 'mp')  107 us
    reduce_scatter x1, waiting for transfers between devices, body(): lax.psum_scatter(jnp.dot(hidden_act, down_local, preferred_element_type=j...  78.6 us
    psum x1, waiting for transfers between devices, body(): lax.psum(back_part.astype(jnp.bfloat16), ('mp', 'width'))  47.9 us
    all_gather x1, waiting for transfers between devices, body(): gathered = lax.all_gather(residual_in[0], 'hidden', axis=0, tiled=True)  47 us
    reduce_scatter x1, waiting for transfers between devices, body(): lax.psum_scatter(recon_part, 'hidden', scatter_dimension=0, tiled=True)  45.1 us
    all_gather x1, waiting for transfers between devices, body(): lax.all_gather(mlp_acts, 'hidden', axis=0, tiled=True).astype(jnp.float32)  27 us
    dot_general x1, matrix products, body(): recon_part = jnp.dot(latents, dec_weight, precision=highest)  26.6 us
  transfers between devices with their start and end apart: 9, of which 9 were waited for; matrix products, arithmetic and copies ran while one was open for 4% of the time, Pallas kernels for 0%

profile of v1, /device:TPU:0, one launch (start us, length us, event | category | flops | bytes accessed | tf_op | source)
XLA Modules:
  0.0 663.3 jit_solution(14955147231079574819)
XLA Ops:
  7.2 0.0 all-gather.9.cloned.1.call-start
  7.2 0.7 all-gather.9.cloned.1.call-update
  7.9 0.0 reduce-scatter.4.cloned.1.call-start
  7.9 47.0 %all-gather.9.cloned.1.call-done = bf16[1,512,3584]{2,1,0:T(8,128)(2,1)} async-done(((bf16[1,64,3584]{2,1,0:T(8,128)(2,1)}), bf16[1,512,3584]{2,1,0:T(8,128)(2,1)}) %all-gather.9.cloned.1.call-update) | async-done | bytes 3670032 | tf_op jit(solution)/shard_map/all_gather | solution.py:18
  54.9 9.6 %fusion.4 = f32[512,896]{1,0:T(8,128)S(1)} fusion(bf16[1,896,3584]{2,1,0:T(8,128)(2,1)} %param.9, bf16[1,512,3584]{2,1,0:T(8,128)(2,1)} %all-gather.9.cloned.1.call-done), kind=kOutput, calls=%fused_computation.7 | convolution fusion | flops 3288334336 | bytes 11927552 | tf_op jit(solution)/shard_map/dot_general | solution.py:19
  64.6 0.0 slice-start.1
  64.6 7.1 %fusion.17 = bf16[512,896]{1,0:T(8,128)(2,1)S(1)} fusion(f32[512,896]{1,0:T(8,128)S(1)} %fusion.4, bf16[1,896,3584]{2,1,0:T(8,128)(2,1)} %param.10, bf16[1,512,3584]{2,1,0:T(8,128)(2,1)S(1)} %copy-done.7), kind=kOutput, calls=%fused_computation.25 | convolution fusion | flops 3292921856 | bytes 12845056 | tf_op jit(solution)/shard_map/dot_general | solution.py:22
  71.7 6.0 fusion
  77.8 0.0 reduce-scatter.4.cloned.1.call-update
  77.8 0.0 reduce-scatter.6.cloned.1.call-start
  77.9 78.6 %reduce-scatter.4.cloned.1.call-done = f32[64,3584]{1,0:T(8,128)} async-done(((f32[512,3584]{1,0:T(8,128)}), f32[64,3584]{1,0:T(8,128)}) %reduce-scatter.4.cloned.1.call-update) | async-done | bytes 917520 | tf_op jit(solution)/shard_map/reduce_scatter | solution.py:25
  156.4 0.0 reduce-scatter.6.cloned.1.call-update
  156.4 0.0 all-gather.5.cloned.1.call-start
  156.5 19.6 %reduce-scatter.6.cloned.1.call-done = f32[64,1792]{1,0:T(8,128)} async-done(((f32[64,3584]{1,0:T(8,128)}), f32[64,1792]{1,0:T(8,128)}) %reduce-scatter.6.cloned.1.call-update) | async-done | bytes 458768 | tf_op jit(solution)/shard_map/reduce_scatter | solution.py:31
  176.1 1.7 convert_element_type.23
  177.8 0.0 all-gather.5.cloned.1.call-update
  177.9 0.3 all-reduce.4.cloned.1.call-start
  178.2 27.0 %all-gather.5.cloned.1.call-done = bf16[512,1792]{1,0:T(8,128)(2,1)} async-done(((bf16[64,1792]{1,0:T(8,128)(2,1)}), bf16[512,1792]{1,0:T(8,128)(2,1)}) %all-gather.5.cloned.1.call-update) | async-done | bytes 1835024 | tf_op jit(solution)/shard_map/all_gather | solution.py:33
  205.2 16.9 %fusion.26 = f32[512,2048]{1,0:T(8,128)} fusion(bf16[512,1792]{1,0:T(8,128)(2,1)} %all-gather.5.cloned.1.call-done, f32[1792,2048]{1,0:T(8,128)} %param.12), kind=kOutput, calls=%fused_computation.36 | convolution fusion | flops 22548578304 | bytes 20709376 | tf_op jit(solution)/shard_map/dot_general | solution.py:34
  222.1 0.0 all-reduce.4.cloned.1.call-update
  222.1 0.0 all-reduce.6.cloned.1.call-start
  222.2 107.4 %all-reduce.4.cloned.1.call-done = f32[512,2048]{1,0:T(8,128)} async-done(((f32[512,2048]{1,0:T(8,128)}), f32[512,2048]{1,0:T(8,128)}) %all-reduce.4.cloned.1.call-update) | async-done | bytes 4194320 | tf_op jit(solution)/shard_map/psum | solution.py:38
  329.6 0.0 all-reduce.6.cloned.1.call-update
  329.6 0.4 reduce-scatter.8.cloned.1.call-start
  330.0 109.9 %all-reduce.6.cloned.1.call-done = f32[512,2048]{1,0:T(8,128)} async-done(((f32[512,2048]{1,0:T(8,128)}), f32[512,2048]{1,0:T(8,128)}) %all-reduce.6.cloned.1.call-update) | async-done | bytes 4194320 | tf_op jit(solution)/shard_map/psum | solution.py:38
  439.9 4.9 fusion.24
  444.8 0.0 copy-start
  444.8 2.0 copy-done
  446.8 26.6 %fusion.27 = f32[512,1792]{1,0:T(8,128)} fusion(f32[512,2048]{1,0:T(8,128)S(1)} %get-tuple-element.7, f32[2048,1792]{1,0:T(8,128)} %param.14), kind=kOutput, calls=%fused_computation.37 | convolution fusion | flops 22548578304 | bytes 22544384 | tf_op jit(solution)/shard_map/dot_general | solution.py:42
  473.4 0.0 reduce-scatter.8.cloned.1.call-update
  473.5 0.0 all-gather.7.cloned.1.call-start
  473.5 45.1 %reduce-scatter.8.cloned.1.call-done = f32[64,1792]{1,0:T(8,128)} async-done(((f32[512,1792]{1,0:T(8,128)}), f32[64,1792]{1,0:T(8,128)}) %reduce-scatter.8.cloned.1.call-update) | async-done | bytes 458768 | tf_op jit(solution)/shard_map/reduce_scatter | solution.py:43
  518.6 1.8 multiply_convert_fusion
  520.3 0.0 all-gather.7.cloned.1.call-update
  520.4 0.0 all-reduce.8.cloned.1.call-start
  520.4 6.2 multiply_reduce_fusion
  526.6 0.1 broadcast_select_fusion
  526.7 8.1 %psum.38 = f32[2,2048]{1,0:T(2,128)S(1)} all-reduce(f32[2,2048]{1,0:T(2,128)S(1)} %broadcast_select_fusion), channel_id=1, replica_groups=mesh['mp'=2,'width'=2,'hidden'=8] {'mp'}, use_global_device_ids=true, to_apply=%region_7.8 | all-reduce | flops 4096 | bytes 32768 | tf_op jit(solution)/shard_map/psum | solution.py:38
  534.9 8.7 %psum.39 = f32[2,2048]{1,0:T(2,128)S(1)} all-reduce(f32[2,2048]{1,0:T(2,128)S(1)} %psum.38), channel_id=1, replica_groups=mesh['mp'=2,'width'=2,'hidden'=8] {'width'}, use_global_device_ids=true, to_apply=%region_8.9 | all-reduce | flops 4096 | bytes 32768 | tf_op jit(solution)/shard_map/psum | solution.py:38
  543.6 2.6 all-gather.7.cloned.1.call-done
  546.2 18.4 %convolution_convert_fusion = bf16[512,2048]{1,0:T(8,128)(2,1)} fusion(bf16[512,1792]{1,0:T(8,128)(2,1)} %all-gather.7.cloned.1.call-done, f32[2048,1792]{1,0:T(8,128)} %param.14), kind=kOutput, calls=%fused_computation.15 | convolution fusion | flops 22549626880 | bytes 18612224 | tf_op jit(solution)/shard_map/dot_general | solution.py:49
  564.6 0.0 all-reduce.8.cloned.1.call-update
  564.6 0.7 convert_bitcast_fusion
  565.3 0.9 convert_reduce_fusion
  566.2 19.6 %multiply_add_fusion = f32[2048,1792]{1,0:T(8,128)} fusion(f32[2048,1792]{1,0:T(8,128)} %param.14, f32[512,2048]{1,0:T(8,128)} %copy-done, bf16[512,1792]{1,0:T(8,128)(2,1)S(1)} %copy-done.2, f32[2048]{0:T(1024)S(1)} %divide_multiply_fusion.1), kind=kOutput, calls=%fused_computation | convolution fusion | flops 22555918336 | bytes 35397632 | tf_op jit(solution)/shard_map/dot_general | solution.py:62
  585.8 47.9 %all-reduce.8.cloned.1.call-done = bf16[512,2048]{1,0:T(8,128)(2,1)} async-done(((bf16[512,2048]{1,0:T(8,128)(2,1)}), bf16[512,2048]{1,0:T(8,128)(2,1)}) %all-reduce.8.cloned.1.call-update) | async-done | bytes 2097168 | tf_op jit(solution)/shard_map/psum | solution.py:52
  633.7 5.0 fusion.22
  638.6 17.9 %fusion.23 = f32[1792,2048]{1,0:T(8,128)} fusion(bf16[512,1792]{1,0:T(8,128)(2,1)} %all-gather.5.cloned.1.call-done, bf16[512,2048]{1,0:T(8,128)(2,1)S(1)} %copy-done.4, f32[512,2048]{1,0:T(8,128)S(1)} %copy-done.1, f32[2048]{0:T(1024)S(1)} %bitcast.33, f32[2048]{0:T(1024)S(1)} %copy-done.5), kind=kOutput, calls=%fused_computation.34 | convolution fusion | flops 22556966912 | bytes 22822912 | tf_op jit(solution)/shard_map/dot_general | solution.py:57
  (22 shorter events, 0.1 us)
Async XLA Ops:
  7.2 47.7 %all-gather.9.cloned.1.call-start = ((), (), s32[]{:S(2)}) async-start(), calls=%async_computation.11 | async-start | bytes 4128768 | tf_op jit(solution)/shard_map/all_gather | solution.py:18
  7.9 148.5 %reduce-scatter.4.cloned.1.call-start = ((), (), s32[]{:S(2)}) async-start(), calls=%async_computation.3 | async-start | bytes 8257536 | tf_op jit(solution)/shard_map/reduce_scatter | solution.py:25
  54.9 9.6 %copy-start.7 = (bf16[1,512,3584]{2,1,0:T(8,128)(2,1)S(1)}, bf16[1,512,3584]{2,1,0:T(8,128)(2,1)}, u32[]{:S(2)}) copy-start(bf16[1,512,3584]{2,1,0:T(8,128)(2,1)} %all-gather.9.cloned.1.call-done) | copy-start | bytes 11010052
  54.9 16.8 %slice-start = ((s8[6422528]{0:T(1024)(128)(4,1)}), s8[4194304]{0:T(1024)(128)(4,1)S(1)}, s32[]{:S(2)}) async-start(s8[6422528]{0:T(1024)(128)(4,1)} %bitcast.35), calls=%async_computation.12 | async-start | bytes 8388608
  64.6 7.2 %slice-start.1 = ((s8[6422528]{0:T(1024)(128)(4,1)}), s8[2228224]{0:T(1024)(128)(4,1)S(1)}, s32[]{:S(2)}) async-start(s8[6422528]{0:T(1024)(128)(4,1)} %bitcast.35), calls=%async_computation.13 | async-start | bytes 4456448
  77.8 98.3 %reduce-scatter.6.cloned.1.call-start = ((), (), s32[]{:S(2)}) async-start(), calls=%async_computation.4 | async-start | bytes 1376256 | tf_op jit(solution)/shard_map/reduce_scatter | solution.py:31
  156.4 48.8 %all-gather.5.cloned.1.call-start = ((), (), s32[]{:S(2)}) async-start(), calls=%async_computation.5 | async-start | bytes 2064384 | tf_op jit(solution)/shard_map/all_gather | solution.py:33
  177.9 151.7 %all-reduce.4.cloned.1.call-start = ((), (), s32[]{:S(2)}) async-start(), calls=%async_computation.6 | async-start | bytes 8388608 | tf_op jit(solution)/shard_map/psum | solution.py:38
  222.1 217.8 %copy-start.5 = (f32[2048]{0:T(1024)S(1)}, f32[2048]{0:T(1024)}, u32[]{:S(2)}) copy-start(f32[2048]{0:T(1024)} %param.13) | copy-start | bytes 24580
  222.1 217.8 %all-reduce.6.cloned.1.call-start = ((), (), s32[]{:S(2)}) async-start(), calls=%async_computation.7 | async-start | bytes 8388608 | tf_op jit(solution)/shard_map/psum | solution.py:38
  329.6 188.9 %reduce-scatter.8.cloned.1.call-start = ((), (), s32[]{:S(2)}) async-start(), calls=%async_computation.8 | async-start | bytes 4128768 | tf_op jit(solution)/shard_map/reduce_scatter | solution.py:43
  444.8 2.0 copy-start
  446.8 71.8 %copy-start.3 = (f32[64,1792]{1,0:T(8,128)S(1)}, f32[64,1792]{1,0:T(8,128)}, u32[]{:S(2)}) copy-start(f32[64,1792]{1,0:T(8,128)} %reduce-scatter.6.cloned.1.call-done) | copy-start | bytes 1376260
  446.8 71.8 %copy-start.6 = (f32[1792]{0:T(1024)S(1)}, f32[1792]{0:T(1024)}, u32[]{:S(2)}) copy-start(f32[1792]{0:T(1024)} %param.15) | copy-start | bytes 21508
  473.5 72.7 %all-gather.7.cloned.1.call-start = ((), (), s32[]{:S(2)}) async-start(), calls=%async_computation.9 | async-start | bytes 2064384 | tf_op jit(solution)/shard_map/all_gather | solution.py:45
  520.4 113.3 %all-reduce.8.cloned.1.call-start = ((), (), s32[]{:S(2)}) async-start(), calls=%async_computation.10 | async-start | bytes 4194304 | tf_op jit(solution)/shard_map/psum | solution.py:52
  546.2 19.1 %copy-start.2 = (bf16[512,1792]{1,0:T(8,128)(2,1)S(1)}, bf16[512,1792]{1,0:T(8,128)(2,1)}, u32[]{:S(2)}) copy-start(bf16[512,1792]{1,0:T(8,128)(2,1)} %all-gather.7.cloned.1.call-done) | copy-start | bytes 5505028
  633.7 5.0 copy-start.1
  633.7 5.0 copy-start.4
Sparse Core Ops, SparseCore 0:
  9.6 45.2 all-gather.8
  77.9 78.4 reduce-scatter.3
  158.7 17.3 reduce-scatter.5
  178.2 26.9 all-gather.4
  222.2 107.3 all-reduce.3
  331.9 107.9 all-reduce.5
  473.6 44.9 reduce-scatter.7
  520.8 25.3 all-gather.6
  564.7 68.8 all-reduce.7
